TPU v7x, 256 devices: a whole 4x4x8 slice. The times are simulated.
256 devices in a mesh: store: 16 (over y, x_hi, core), dept: 16 (over z, x_lo).
Axes of the slice: x: 4 (x_hi: 2, x_lo: 2; x = x_hi * 2 + x_lo), y: 4, z: 8, core: 2. Of those that a mesh axis runs over, the one named last changes fastest.
Arguments:
- history: bfloat16 [4096, 384, 512], P('store', 'dept'), may hold values from -400 to 400, as said below
- input_layer_matrix: bfloat16 [512, 512], replicated, may hold values from -0.375 to 0.375
- middle_layer_matrix: bfloat16 [512, 512], replicated, may hold values from -0.375 to 0.375
- final_layer_matrix: bfloat16 [512, 28], replicated, may hold values from -0.375 to 0.375
Outputs:
- reconciled: float32 [4096, 10752], P('store', 'dept')
- store_gap: float32 [28, 4096], P(None, 'store')
- item_gap: float32 [28, 384], P(None, 'dept')
Inputs may be any that keep to these rules, and one draw needn't show every extreme that they name: `history`: daily sales histories.
All inputs are finite; a program needn't handle non-finite values.
Results may differ from a plain program's by a relative error of at most 0.0065.
The roundings to bfloat16 on the way count: a program that leaves them out, or rounds other values in their place, can miss the bound.
Values sent between devices are 32-bit elements; how exact they have to be, the bound alone decides.
No kernel may reach another device: no remote copies, remote signals or barrier semaphores. Data moves between devices by JAX's collectives and lax.ppermute only.
A program may use at most 64 MiB of HBM per device.

v0:
```python
import math
import jax
import jax.numpy as jnp
from jax import lax
from jax.sharding import PartitionSpec as P


def predictor_function(sequence_grid, input_layer_matrix, middle_layer_matrix, final_layer_matrix):
    values = sequence_grid.astype(jnp.float32)
    root_mean = jnp.sqrt(jnp.mean(values * values, axis=-1, keepdims=True) + 1e-05)
    scaled = (values / root_mean).astype(jnp.bfloat16)
    hidden_one = jax.nn.relu(
        jnp.dot(scaled, input_layer_matrix, preferred_element_type=jnp.float32)
    ).astype(jnp.bfloat16)
    hidden_two = jax.nn.relu(
        jnp.dot(hidden_one, middle_layer_matrix, preferred_element_type=jnp.float32)
    ).astype(jnp.bfloat16)
    return jnp.dot(hidden_two, final_layer_matrix, preferred_element_type=jnp.float32) * root_mean


def body(history, input_layer_matrix, middle_layer_matrix, final_layer_matrix):
    store_row_set, item_columns, history_count = history.shape
    horizon = final_layer_matrix.shape[1]
    widened_entries = history.astype(jnp.float32)
    store_part = jnp.sum(widened_entries, axis=1)
    item_part = jnp.sum(widened_entries, axis=0)
    product_past_sales = lax.psum(item_part, "store")
    outlet_past_sales = lax.psum(store_part, "dept")
    outlet_estimate = predictor_function(
        outlet_past_sales, input_layer_matrix, middle_layer_matrix, final_layer_matrix
    )
    product_estimate = predictor_function(
        product_past_sales, input_layer_matrix, middle_layer_matrix, final_layer_matrix
    )
    finest_tier = predictor_function(
        history.reshape(store_row_set * item_columns, history_count),
        input_layer_matrix,
        middle_layer_matrix,
        final_layer_matrix,
    )
    finest_tier = finest_tier.reshape(store_row_set, item_columns, horizon)
    row_part = jnp.sum(finest_tier, axis=1)
    col_part = jnp.sum(finest_tier, axis=0)
    row_sum = lax.psum(row_part, "dept")
    col_sum = lax.psum(col_part, "store")
    store_err = outlet_estimate - row_sum
    item_err = product_estimate - col_sum
    err_s = lax.psum(jnp.sum(store_err, axis=0), "store")
    err_i = lax.psum(jnp.sum(item_err, axis=0), "dept")
    item_count = float(item_columns * lax.axis_size("dept"))
    store_count = float(store_row_set * lax.axis_size("store"))
    denominator = 1.0 + item_count + store_count
    shift_s = (err_s * (1.0 + store_count) - store_count * err_i) / denominator
    shift_i = ((1.0 + item_count) * err_i - item_count * err_s) / denominator
    store_shift = (store_err - shift_i) / (1.0 + item_count)
    item_shift = (item_err - shift_s) / (1.0 + store_count)
    reconciled = finest_tier + store_shift[:, None, :] + item_shift[None, :, :]
    store_gap = (store_err / math.sqrt(item_count)).T
    item_gap = (item_err / math.sqrt(store_count)).T
    return (reconciled.reshape(store_row_set, item_columns * horizon), store_gap, item_gap)


def solution(mesh):
    return jax.shard_map(
        body,
        mesh=mesh,
        in_specs=(P("store", "dept", None), P(), P(), P()),
        out_specs=(P("store", "dept"), P(None, "store"), P(None, "dept")),
        check_vma=False,
    )
```

profile of v0, /device:TPU:1, one launch (start us, length us, event | category | flops | bytes accessed | tf_op | source)
XLA Modules:
  0.0 231.8 jit_solution(3153932601823036586)
XLA Ops:
  7.2 0.0 copy-start
  7.2 0.0 all-reduce.4.cloned.1.call-start
  7.2 6.6 %convert_reduce_fusion = (f32[24,512]{1,0:T(8,128)S(1)}, f32[256,24]{1,0:T(8,128)S(1)}, f32[256,512]{1,0:T(8,128)}) fusion(bf16[256,24,512]{2,1,0:T(8,128)(2,1)} %param.4), kind=kLoop, calls=%fused_computation.5 | loop fusion | flops 15579136 | bytes 6889472 | tf_op jit(solution)/shard_map/reduce_sum | solution.py:26
  13.8 0.0 all-reduce.4.cloned.1.call-update
  13.9 0.1 sqrt.28
  14.0 0.0 copy-start.1
  14.0 7.2 %fusion = bf16[6144,512]{1,0:T(8,128)(2,1)} fusion(bf16[256,24,512]{2,1,0:T(8,128)(2,1)} %param.4, f32[6144]{0:T(1024)S(1)} %sqrt.28), kind=kLoop, calls=%fused_computation.1 | loop fusion | flops 9437184 | bytes 12607488 | tf_op jit(solution)/shard_map/convert_element_type | solution.py:11
  21.3 0.0 copy-done
  21.3 10.4 %maximum_convert_fusion = bf16[6144,512]{1,0:T(8,128)(2,1)} fusion(bf16[512,512]{1,0:T(8,128)(2,1)S(1)} %copy-done, bf16[6144,512]{1,0:T(8,128)(2,1)} %fusion, bf16[512,512]{1,0:T(8,128)(2,1)S(1)} %copy-done.1), kind=kOutput, calls=%fused_computation.2 | convolution fusion | flops 6455033856 | bytes 13631488 | tf_op jit(solution)/shard_map/dot_general | solution.py:16
  31.7 4.7 %convolution_multiply_fusion = f32[6144,28]{0,1:T(8,128)S(1)} fusion(bf16[6144,512]{1,0:T(8,128)(2,1)} %maximum_convert_fusion, bf16[512,28]{0,1:T(8,128)(2,1)S(1)} %copy-done.2, f32[6144]{0:T(1024)S(1)} %sqrt.28), kind=kOutput, calls=%fused_computation.7 | convolution fusion | flops 176332800 | bytes 7032832 | tf_op jit(solution)/shard_map/dot_general | solution.py:18
  36.4 4.4 %reshape.57 = f32[256,24,28]{1,0,2:T(8,128)} reshape(f32[6144,28]{0,1:T(8,128)S(1)} %convolution_multiply_fusion) | data formatting | bytes 1376256 | tf_op jit(solution)/shard_map/reshape | solution.py:41
  40.8 3.1 %fusion.17 = (f32[24,28]{0,1:T(8,128)S(1)}, f32[256,28]{0,1:T(8,128)S(1)}) fusion(f32[256,24,28]{1,0,2:T(8,128)} %reshape.57), kind=kLoop, calls=%fused_computation.42 | loop fusion | flops 336224 | bytes 719488 | tf_op jit(solution)/shard_map/reduce_sum | solution.py:43
  43.9 0.1 copy.15
  44.0 65.5 %all-reduce.1 = (f32[24,28]{1,0:T(8,128)S(1)}, f32[24,512]{1,0:T(8,128)S(1)}) all-reduce(f32[24,28]{1,0:T(8,128)S(1)} %copy.15, f32[24,512]{1,0:T(8,128)S(1)} %get-tuple-element.12), channel_id=1, replica_groups=mesh['store'=16,'dept'=16] {'store'}, use_global_device_ids=true, to_apply=%region_10.11 | all-reduce | flops 12960 | bytes 103680 | tf_op jit(solution)/shard_map/psum | solution.py:45
  109.5 0.1 multiply_reduce_fusion.2
  109.6 2.2 copy.14
  111.8 2.4 %reshape.56 = f32[256,672]{1,0:T(8,128)S(1)} reshape(f32[6144,28]{1,0:T(8,128)} %copy.14) | data formatting | bytes 1376256 | tf_op jit(solution)/shard_map/reshape | solution.py:41
  114.3 0.4 fusion.5
  114.6 0.2 fusion.18
  114.8 53.4 %all-reduce = (f32[256,28]{0,1:T(8,128)S(1)}, f32[28]{0:T(128)S(1)}) all-reduce(f32[256,28]{0,1:T(8,128)S(1)} %get-tuple-element.16, f32[28]{0:T(128)S(1)} %get-tuple-element.27), channel_id=1, replica_groups=mesh['store'=16,'dept'=16] {'dept'}, use_global_device_ids=true, to_apply=%region_5.6 | all-reduce | flops 7196 | bytes 57568 | tf_op jit(solution)/shard_map/psum | solution.py:44
  168.2 1.2 multiply_reduce_fusion.1
  169.4 1.6 fusion.3
  171.0 0.3 fusion.19
  171.3 50.7 %psum.47 = f32[28]{0:T(128)S(1)} all-reduce(f32[28]{0:T(128)S(1)} %get-tuple-element.29), channel_id=1, replica_groups=mesh['store'=16,'dept'=16] {'store'}, use_global_device_ids=true, to_apply=%region_14.15 | all-reduce | flops 28 | bytes 224 | tf_op jit(solution)/shard_map/psum | solution.py:48
  222.0 0.6 multiply_bitcast_fusion.1
  222.6 0.1 add.73
  222.7 0.6 multiply_bitcast_fusion
  223.3 0.1 add.70
  223.4 0.1 add.71
  223.5 0.3 copy.16
  223.8 0.1 add_add_fusion
  223.9 1.1 copy.17
  (8 shorter events, 0.1 us)
Async XLA Ops:
  7.2 14.1 %copy-start = (bf16[512,512]{1,0:T(8,128)(2,1)S(1)}, bf16[512,512]{1,0:T(8,128)(2,1)}, u32[]{:S(2)}) copy-start(bf16[512,512]{1,0:T(8,128)(2,1)} %param.6) | copy-start | bytes 1572868
  7.2 161.0 %all-reduce.4.cloned.1.call-start = ((), (), s32[]{:S(2)}) async-start(), calls=%async_computation | async-start | bytes 1048576 | tf_op jit(solution)/shard_map/psum | solution.py:28
  14.0 7.3 %copy-start.1 = (bf16[512,512]{1,0:T(8,128)(2,1)S(1)}, bf16[512,512]{1,0:T(8,128)(2,1)}, u32[]{:S(2)}) copy-start(bf16[512,512]{1,0:T(8,128)(2,1)} %param.5) | copy-start | bytes 1572868
  21.3 10.4 %copy-start.2 = (bf16[512,28]{0,1:T(8,128)(2,1)S(1)}, bf16[512,28]{0,1:T(8,128)(2,1)}, u32[]{:S(2)}) copy-start(bf16[512,28]{0,1:T(8,128)(2,1)} %param.7) | copy-start | bytes 86020
Sparse Core Ops, SparseCore 0:
  14.0 130.8 all-reduce.3
where the time goes:
time: 232 us
  blocking collectives  170 us (73%)
  other arithmetic  19.6 us (8%)
  matrix products  17.5 us (8%)
  between operations  14.1 us (6%)
  local copies, waits for them, and re-layouts  10.9 us (5%)
    psum x1, blocking collectives, body(): col_sum = lax.psum(col_part, 'store')  65.5 us
    psum x1, blocking collectives, body(): row_sum = lax.psum(row_part, 'dept')  53.4 us
    psum x1, blocking collectives, body(): err_s = lax.psum(jnp.sum(store_err, axis=0), 'store')  50.7 us
    dot_general x3, matrix products, predictor_function(): jnp.dot(hidden_one, middle_layer_matrix, preferred_element_type=jnp.float32)  12.4 us
    convert_element_type x1, other arithmetic, predictor_function(): scaled = (values / root_mean).astype(jnp.bfloat16)  7.24 us
    reshape x2, local copies, waits for them, and re-layouts, body(): finest_tier = finest_tier.reshape(store_row_set, item_columns, horizon)  6.88 us
    reduce_sum x1, other arithmetic, body(): item_part = jnp.sum(widened_entries, axis=0)  6.59 us
    dot_general x3, matrix products, predictor_function(): jnp.dot(hidden_two, final_layer_matrix, preferred_element_type=jnp.float32)  5.15 us
  transfers between devices with their start and end apart: 1, of which 0 were waited for; matrix products, arithmetic and copies ran while one was open for 15% of the time, Pallas kernels for 0%

commit v1 on v0

--- a/solution.py
+++ b/solution.py
@@ -41,7 +41,7 @@
     finest_tier = finest_tier.reshape(store_row_set, item_columns, horizon)
     row_part = jnp.sum(finest_tier, axis=1)
     col_part = jnp.sum(finest_tier, axis=0)
-    row_sum = lax.psum(row_part, "dept")
+    row_sum = jnp.sum(lax.all_gather(row_part, "dept"), axis=0)
     col_sum = lax.psum(col_part, "store")
     store_err = outlet_estimate - row_sum
     item_err = product_estimate - col_sum

time: 232 us -> 266 us (1.15)
  the two profiles are of different devices: /device:TPU:1 before, /device:TPU:0 now
where the time goes in v1:
time: 266 us; the launch traced here: 265 us
  blocking collectives  137 us (52%)
  waiting for transfers between devices  65.4 us (25%)
  other arithmetic  19.8 us (7%)
  matrix products  17.6 us (7%)
  between operations  14.1 us (5%)
  local copies, waits for them, and re-layouts  11.1 us (4%)
    psum x1, waiting for transfers between devices, body(): outlet_past_sales = lax.psum(store_part, 'dept')  65.4 us
    psum x1, blocking collectives, body(): err_s = lax.psum(jnp.sum(store_err, axis=0), 'store')  65 us
    all_gather x1, blocking collectives, body(): row_sum = jnp.sum(lax.all_gather(row_part, 'dept'), axis=0)  37.9 us
    psum x1, blocking collectives, body(): err_i = lax.psum(jnp.sum(item_err, axis=0), 'dept')  34.3 us
    dot_general x3, matrix products, predictor_function(): jnp.dot(hidden_one, middle_layer_matrix, preferred_element_type=jnp.float32)  12.4 us
    convert_element_type x1, other arithmetic, predictor_function(): scaled = (values / root_mean).astype(jnp.bfloat16)  7.36 us
    reshape x2, local copies, waits for them, and re-layouts, body(): finest_tier = finest_tier.reshape(store_row_set, item_columns, horizon)  6.86 us
    reduce_sum x1, other arithmetic, body(): item_part = jnp.sum(widened_entries, axis=0)  6.59 us
  transfers between devices with their start and end apart: 1, of which 1 were waited for; matrix products, arithmetic and copies ran while one was open for 13% of the time, Pallas kernels for 0%

profile of v1, /device:TPU:0, one launch (start us, length us, event | category | flops | bytes accessed | tf_op | source)
XLA Modules:
  0.0 265.3 jit_solution(12750152055746011380)
XLA Ops:
  7.2 0.0 all-reduce.3.cloned.1.call-start
  7.2 6.6 %convert_reduce_fusion = (f32[24,512]{1,0:T(8,128)S(1)}, f32[256,24]{1,0:T(8,128)S(1)}, f32[256,512]{1,0:T(8,128)}) fusion(bf16[256,24,512]{2,1,0:T(8,128)(2,1)} %param.4), kind=kLoop, calls=%fused_computation.5 | loop fusion | flops 15579136 | bytes 6889472 | tf_op jit(solution)/shard_map/reduce_sum | solution.py:26
  13.8 0.0 all-reduce.3.cloned.1.call-update
  13.9 0.1 sqrt.28
  14.0 7.4 %fusion = bf16[6144,512]{1,0:T(8,128)(2,1)} fusion(bf16[256,24,512]{2,1,0:T(8,128)(2,1)} %param.4, f32[6144]{0:T(1024)S(1)} %sqrt.28), kind=kLoop, calls=%fused_computation.1 | loop fusion | flops 9437184 | bytes 12607488 | tf_op jit(solution)/shard_map/convert_element_type | solution.py:11
  21.4 10.4 %maximum_convert_fusion = bf16[6144,512]{1,0:T(8,128)(2,1)} fusion(bf16[512,512]{1,0:T(8,128)(2,1)S(1)} %copy-done, bf16[6144,512]{1,0:T(8,128)(2,1)} %fusion, bf16[512,512]{1,0:T(8,128)(2,1)S(1)} %copy-done.1), kind=kOutput, calls=%fused_computation.2 | convolution fusion | flops 6455033856 | bytes 13631488 | tf_op jit(solution)/shard_map/dot_general | solution.py:16
  31.8 4.7 %convolution_multiply_fusion = f32[6144,28]{0,1:T(8,128)S(1)} fusion(bf16[6144,512]{1,0:T(8,128)(2,1)} %maximum_convert_fusion, bf16[512,28]{0,1:T(8,128)(2,1)S(1)} %copy-done.2, f32[6144]{0:T(1024)S(1)} %sqrt.28), kind=kOutput, calls=%fused_computation.7 | convolution fusion | flops 176332800 | bytes 7032832 | tf_op jit(solution)/shard_map/dot_general | solution.py:18
  36.5 2.3 copy.14
  38.8 4.4 %reshape.57 = f32[256,24,28]{1,0,2:T(8,128)} reshape(f32[6144,28]{0,1:T(8,128)S(1)} %convolution_multiply_fusion) | data formatting | bytes 1376256 | tf_op jit(solution)/shard_map/reshape | solution.py:41
  43.3 2.4 reshape.56
  45.7 3.1 %fusion.17 = (f32[24,28]{0,1:T(8,128)S(1)}, f32[256,28]{0,1:T(8,128)S(1)}) fusion(f32[256,24,28]{1,0,2:T(8,128)} %reshape.57), kind=kLoop, calls=%fused_computation.43 | loop fusion | flops 336224 | bytes 719488 | tf_op jit(solution)/shard_map/reduce_sum | solution.py:43
  48.8 0.1 copy.15
  48.8 37.9 %all-gather = f32[4096,28]{0,1:T(8,128)S(1)} all-gather(f32[256,28]{0,1:T(8,128)S(1)} %get-tuple-element.16), channel_id=2, replica_groups=mesh['store'=16,'dept'=16] {'dept'}, dimensions={0}, use_global_device_ids=true | all-gather | bytes 487424 | tf_op jit(solution)/shard_map/all_gather | solution.py:44
  86.8 0.2 copy.18
  86.9 0.1 bitcast_reduce_fusion
  87.0 65.4 %all-reduce.3.cloned.1.call-done = f32[256,512]{1,0:T(8,128)} async-done(((f32[256,512]{1,0:T(8,128)}), f32[256,512]{1,0:T(8,128)}) %all-reduce.3.cloned.1.call-update) | async-done | bytes 524304 | tf_op jit(solution)/shard_map/psum | solution.py:28
  152.5 1.2 multiply_reduce_fusion.1
  153.6 1.6 fusion.3
  155.2 0.3 fusion.18
  155.5 65.0 %all-reduce = (f32[28]{0:T(128)S(1)}, f32[24,28]{1,0:T(8,128)S(1)}, f32[24,512]{1,0:T(8,128)S(1)}) all-reduce(f32[28]{0:T(128)S(1)} %get-tuple-element.26, f32[24,28]{1,0:T(8,128)S(1)} %copy.15, f32[24,512]{1,0:T(8,128)S(1)} %get-tuple-element.12), channel_id=1, replica_groups=mesh['store'=16,'dept'=16] {'store'}, use_global_device_ids=true, to_apply=%region_14.15 | all-reduce | flops 12988 | bytes 103904 | tf_op jit(solution)/shard_map/psum | solution.py:48
  220.6 0.1 multiply_reduce_fusion.2
  220.7 0.4 fusion.5
  221.1 0.2 fusion.19
  221.2 34.3 %psum.38 = f32[28]{0:T(128)S(1)} all-reduce(f32[28]{0:T(128)S(1)} %get-tuple-element.28), channel_id=1, replica_groups=mesh['store'=16,'dept'=16] {'dept'}, use_global_device_ids=true, to_apply=%region_12.13 | all-reduce | flops 28 | bytes 224 | tf_op jit(solution)/shard_map/psum | solution.py:49
  255.5 0.6 multiply_bitcast_fusion.1
  256.1 0.1 add.71
  256.2 0.6 multiply_bitcast_fusion
  256.8 0.1 add.68
  256.9 0.1 add.69
  257.0 0.3 copy.16
  257.3 0.1 add_add_fusion
  257.4 1.1 copy.17
  (10 shorter events, 0.1 us)
Async XLA Ops:
  7.2 14.2 %copy-start = (bf16[512,512]{1,0:T(8,128)(2,1)S(1)}, bf16[512,512]{1,0:T(8,128)(2,1)}, u32[]{:S(2)}) copy-start(bf16[512,512]{1,0:T(8,128)(2,1)} %param.6) | copy-start | bytes 1572868
  7.2 145.3 %all-reduce.3.cloned.1.call-start = ((), (), s32[]{:S(2)}) async-start(), calls=%async_computation | async-start | bytes 1048576 | tf_op jit(solution)/shard_map/psum | solution.py:28
  14.0 7.4 %copy-start.1 = (bf16[512,512]{1,0:T(8,128)(2,1)S(1)}, bf16[512,512]{1,0:T(8,128)(2,1)}, u32[]{:S(2)}) copy-start(bf16[512,512]{1,0:T(8,128)(2,1)} %param.5) | copy-start | bytes 1572868
  21.4 10.4 %copy-start.2 = (bf16[512,28]{0,1:T(8,128)(2,1)S(1)}, bf16[512,28]{0,1:T(8,128)(2,1)}, u32[]{:S(2)}) copy-start(bf16[512,28]{0,1:T(8,128)(2,1)} %param.7) | copy-start | bytes 86020
Sparse Core Ops, SparseCore 0:
  14.0 138.4 all-reduce.2
